TPU v7x, 256 devices: a whole 4x4x8 slice. The times are simulated.
256 devices in a mesh: wide: 32 (over x, y, core), narrow: 8 (over z).
Axes of the slice: x: 4, y: 4, z: 8, core: 2. Of those that a mesh axis runs over, the one named last changes fastest.
Arguments:
- panels: float32 [256, 512, 512], P('wide', 'narrow'), may hold values from -0.6 to 0.6
- factors: float32 [64, 512, 512], P('wide', 'narrow'), may hold values from -2 to 2
- member: int32 [64, 4], replicated, may hold values from 0 to 255, as said below
- target: int32 [64, 10], replicated, may hold values from 0 to 31
- ancestors: float32 [32, 512, 512], P('wide', 'narrow'), may hold values from -6 to 6
Outputs:
- updated: float32 [32, 512, 512], P('wide', 'narrow')
Inputs may be any that keep to these rules, and one draw needn't show every extreme that they name: `member`: the blocks of supernode s are 4 distinct indices in [(s // 2) * 8, (s // 2 + 1) * 8); every block belongs to exactly one supernode.
All inputs are finite; a program needn't handle non-finite values.
Results may differ from a plain program's by a relative error of at most 0.0003.
Values sent between devices are 32-bit elements; how exact they have to be, the bound alone decides.
No kernel may reach another device: no remote copies, remote signals or barrier semaphores. Data moves between devices by JAX's collectives and lax.ppermute only.
A program may use at most 128 MiB of HBM per device.

v0:
```python
import jax
import jax.numpy as jnp
import numpy as np
from jax import lax
from jax.sharding import PartitionSpec as P


def pair_lists(count):
    left_pick = []
    right_pick = []
    for upper in range(count):
        for lower in range(upper + 1):
            left_pick.append(upper)
            right_pick.append(lower)
    return (np.array(left_pick, dtype=np.int32), np.array(right_pick, dtype=np.int32))


def shards(panels, factors, member, target, ancestors):
    highest = lax.Precision.HIGHEST
    sup_count = factors.shape[0]
    blk_count = panels.shape[0]
    tile_count = ancestors.shape[0] * lax.axis_size("wide")
    left_pick, right_pick = pair_lists(member.shape[1])
    owner_index = lax.axis_index("wide")
    own_members = (
        lax.dynamic_slice_in_dim(member, owner_index * sup_count, sup_count, 0)
        - owner_index * blk_count
    )
    own_targets = lax.dynamic_slice_in_dim(target, owner_index * sup_count, sup_count, 0)
    full_factors = lax.all_gather(factors, "narrow", axis=1, tiled=True)
    blocks = panels[own_members]
    scaled = jnp.einsum("skrw,swv->skrv", blocks, full_factors, precision=highest)
    left_rows = scaled[:, left_pick]
    right_rows = lax.all_gather(scaled, "narrow", axis=2, tiled=True)[:, right_pick]
    updates = jnp.einsum("sprv,spmv->sprm", left_rows, right_rows, precision=highest)
    tile_ids = jnp.arange(tile_count, dtype=jnp.int32)
    onehot = (own_targets[:, :, None] == tile_ids[None, None, :]).astype(jnp.float32)
    portion = jnp.einsum("spa,sprw->arw", onehot, updates, precision=highest)
    totals = lax.psum_scatter(portion, "wide", scatter_dimension=0, tiled=True)
    return ancestors - totals


def solution(mesh):
    return jax.shard_map(
        shards,
        mesh=mesh,
        in_specs=(
            P("wide", "narrow", None),
            P("wide", "narrow", None),
            P(),
            P(),
            P("wide", "narrow", None),
        ),
        out_specs=P("wide", "narrow", None),
        check_vma=False,
    )
```

profile of v0, /device:TPU:2, one launch (start us, length us, event | category | flops | bytes accessed | tf_op | source)
XLA Modules:
  0.0 293.5 jit_solution(6393277430765025806)
XLA Ops:
  6.5 0.0 copy-start
  6.5 0.0 all-gather.3.cloned.1.call-start
  6.5 0.7 all-gather.3.cloned.1.call-update
  7.3 0.0 all-gather.5.cloned.1.call-start
  7.3 0.8 compare_select_fusion
  8.1 0.1 copy.15
  8.2 0.1 reshape.3
  8.3 0.0 copy-done
  8.3 0.6 gather_fusion
  8.9 44.1 %all-gather.3.cloned.1.call-done = f32[2,512,512]{2,1,0:T(8,128)} async-done(((f32[2,64,512]{2,1,0:T(8,128)}), f32[2,512,512]{2,1,0:T(8,128)}) %all-gather.3.cloned.1.call-update) | async-done | bytes 2097168 | tf_op jit(solution)/shard_map/all_gather | solution.py:30
  53.0 0.0 copy-start.3
  53.0 0.0 copy-start.5
  53.0 0.0 copy-start.4
  53.0 4.5 %fusion.8 = f32[2,4,64,512]{3,2,1,0:T(8,128)} fusion(f32[2,4,64,512]{3,2,1,0:T(8,128)S(1)} %bitcast.21, f32[2,512,512]{2,1,0:T(8,128)} %all-gather.3.cloned.1.call-done), kind=kOutput, calls=%fused_computation.9 | convolution fusion | flops 1610612736 | bytes 4194304 | tf_op jit(solution)/shard_map/skrw,swv->skrv/dot_general | solution.py:32
  57.5 0.0 copy-start.1
  57.5 0.0 all-gather.5.cloned.1.call-update
  57.6 0.0 reduce-scatter.2.cloned.1.call-start
  57.6 0.0 copy-done.3
  57.6 0.1 constant_dynamic-slice_fusion
  57.7 0.1 copy.14
  57.8 0.0 copy-done.5
  57.8 0.0 copy-done.4
  57.8 0.9 copy-done.1
  58.8 2.2 gather_fusion.1
  60.9 89.4 %all-gather.5.cloned.1.call-done = f32[2,4,512,512]{3,2,1,0:T(8,128)} async-done(((f32[2,4,64,512]{3,2,1,0:T(8,128)}), f32[2,4,512,512]{3,2,1,0:T(8,128)}) %all-gather.5.cloned.1.call-update) | async-done | bytes 8388624 | tf_op jit(solution)/shard_map/all_gather | solution.py:34
  150.3 12.6 %gather_fusion.2 = f32[10,2,512,512]{3,2,1,0:T(8,128)} fusion(f32[2,4,512,512]{3,2,1,0:T(8,128)} %all-gather.5.cloned.1.call-done, s32[1024]{0:T(1024)S(1)} %pad_clamp_fusion), kind=kCustom, calls=%fused_computation.2 | custom fusion | bytes 41943080 | tf_op jit(solution)/shard_map/gather | solution.py:34
  162.9 25.8 %fusion = f32[2,10,64,512]{3,2,1,0:T(8,128)S(1)} fusion(f32[10,2,512,512]{3,2,1,0:T(8,128)} %gather_fusion.2, f32[10,2,64,512]{3,2,1,0:T(8,128)} %gather_fusion.1), kind=kOutput, calls=%fused_computation.3 | convolution fusion | flops 4026531840 | bytes 26214400 | tf_op jit(solution)/shard_map/sprv,spmv->sprm/dot_general | solution.py:35
  188.7 3.9 %fusion.5 = f32[32,64,512]{2,0,1:T(8,128)S(1)} fusion(f32[2,10,64,512]{3,2,1,0:T(8,128)S(1)} %fusion, s32[2,10]{1,0:T(2,128)S(1)} %copy.14), kind=kOutput, calls=%fused_computation.8 | convolution fusion | flops 251658880 | bytes 6815824 | tf_op jit(solution)/shard_map/spa,sprw->arw/dot_general | solution.py:38
  192.6 4.4 %copy.16 = f32[32,64,512]{2,1,0:T(8,128)} copy(f32[32,64,512]{2,0,1:T(8,128)S(1)} %fusion.5) | data formatting | bytes 8388608 | tf_op jit(solution)/shard_map/spa,sprw->arw/dot_general | solution.py:38
  197.0 0.0 copy-start.2
  197.0 0.0 reduce-scatter.2.cloned.1.call-update
  197.0 88.4 %reduce-scatter.2.cloned.1.call-done = f32[1,64,512]{2,1,0:T(8,128)} async-done(((f32[32,64,512]{2,1,0:T(8,128)}), f32[1,64,512]{2,1,0:T(8,128)}) %reduce-scatter.2.cloned.1.call-update) | async-done | bytes 131088 | tf_op jit(solution)/shard_map/reduce_scatter | solution.py:39
  285.4 0.0 copy-done.2
  285.4 1.6 sub.11
  (3 shorter events, 0.0 us)
Async XLA Ops:
  6.5 1.7 copy-start
  6.5 46.4 %all-gather.3.cloned.1.call-start = ((), (), s32[]{:S(2)}) async-start(), calls=%async_computation.1 | async-start | bytes 2359296 | tf_op jit(solution)/shard_map/all_gather | solution.py:30
  7.3 143.1 %all-gather.5.cloned.1.call-start = ((), (), s32[]{:S(2)}) async-start(), calls=%async_computation.2 | async-start | bytes 9437184 | tf_op jit(solution)/shard_map/all_gather | solution.py:34
  53.0 4.6 %copy-start.3 = (s32[64,10]{0,1:T(8,128)S(1)}, s32[64,10]{0,1:T(8,128)}, u32[]{:S(2)}) copy-start(s32[64,10]{0,1:T(8,128)} %param.12) | copy-start | bytes 7684
  53.0 4.8 %copy-start.5 = (s32[10]{0:T(128)S(1)}, s32[10]{0:T(128)}, u32[]{:S(2)}) copy-start(s32[10]{0:T(128)} %constant.33) | copy-start | bytes 124
  53.0 4.8 %copy-start.4 = (s32[10]{0:T(128)S(1)}, s32[10]{0:T(128)}, u32[]{:S(2)}) copy-start(s32[10]{0:T(128)} %constant.32) | copy-start | bytes 124
  57.5 1.2 copy-start.1
  57.6 227.9 %reduce-scatter.2.cloned.1.call-start = ((), (), s32[]{:S(2)}) async-start(), calls=%async_computation.3 | async-start | bytes 4325376 | tf_op jit(solution)/shard_map/reduce_scatter | solution.py:39
  197.0 88.4 %copy-start.2 = (f32[1,64,512]{2,1,0:T(8,128)S(1)}, f32[1,64,512]{2,1,0:T(8,128)}, u32[]{:S(2)}) copy-start(f32[1,64,512]{2,1,0:T(8,128)} %param.13) | copy-start | bytes 393220
Sparse Core Ops, SparseCore 0:
  9.1 43.8 all-gather.2
  57.7 92.6 all-gather.4
  197.1 88.2 reduce-scatter.1
where the time goes:
time: 294 us
  waiting for transfers between devices  223 us (76%)
  matrix products  34.2 us (12%)
  local copies, waits for them, and re-layouts  21.1 us (7%)
  between operations  13.2 us (4%)
    all_gather x1, waiting for transfers between devices, shards(): lax.all_gather(scaled, 'narrow', axis=2, tiled=True)[:, right_pick]  89.4 us
    reduce_scatter x1, waiting for transfers between devices, shards(): totals = lax.psum_scatter(portion, 'wide', scatter_dimension=0, tiled=True)  88.4 us
    all_gather x1, waiting for transfers between devices, shards(): full_factors = lax.all_gather(factors, 'narrow', axis=1, tiled=True)  44.1 us
    dot_general x1, matrix products, shards(): jnp.einsum('sprv,spmv->sprm', left_rows, right_rows, precision=highest)  25.8 us
    gather x1, local copies, waits for them, and re-layouts, shards(): lax.all_gather(scaled, 'narrow', axis=2, tiled=True)[:, right_pick]  12.6 us
  transfers between devices with their start and end apart: 3, of which 3 were waited for; matrix products, arithmetic and copies ran while one was open for 1% of the time, Pallas kernels for 0%

commit v1 on v0

--- a/solution.py
+++ b/solution.py
@@ -31,7 +31,9 @@
     blocks = panels[own_members]
     scaled = jnp.einsum("skrw,swv->skrv", blocks, full_factors, precision=highest)
     left_rows = scaled[:, left_pick]
-    right_rows = lax.all_gather(scaled, "narrow", axis=2, tiled=True)[:, right_pick]
+    right_rows = jnp.concatenate(
+        lax.all_to_all(jnp.stack([scaled] * lax.axis_size("narrow")), "narrow", 0, 0), axis=2
+    )[:, right_pick]
     updates = jnp.einsum("sprv,spmv->sprm", left_rows, right_rows, precision=highest)
     tile_ids = jnp.arange(tile_count, dtype=jnp.int32)
     onehot = (own_targets[:, :, None] == tile_ids[None, None, :]).astype(jnp.float32)

time: 294 us -> 398 us (1.35)
  waiting for transfers between devices: 223 us -> 310 us
  local copies, waits for them, and re-layouts: 21.1 us -> 33 us
  starting transfers between devices: 0.08 us -> 5.3 us
    all_to_all x0 -> x1, waiting for transfers between devices: none -> 180 us  [shards(): lax.all_to_all(jnp.stack([scaled] * lax.axis_size('narrow')), 'narrow', 0...]
    all_gather x1 -> x0, waiting for transfers between devices: 89.4 us -> none  [shards(): lax.all_gather(scaled, 'narrow', axis=2, tiled=True)[:, right_pick]]
    all_to_all x0 -> x1, local copies, waits for them, and re-layouts: none -> 8.46 us  [shards(): lax.all_to_all(jnp.stack([scaled] * lax.axis_size('narrow')), 'narrow', 0...]
    all_to_all x0 -> x1, starting transfers between devices: none -> 5.08 us  [shards(): lax.all_to_all(jnp.stack([scaled] * lax.axis_size('narrow')), 'narrow', 0...]
    another operation x0 -> x1, local copies, waits for them, and re-layouts: none -> 4.33 us  [shards(): jnp.stack([scaled] * lax.axis_size('narrow'))]
where the time goes in v1:
time: 398 us
  waiting for transfers between devices  310 us (78%)
  matrix products  33.2 us (8%)
  local copies, waits for them, and re-layouts  33 us (8%)
  between operations  13.5 us (3%)
  starting transfers between devices  5.3 us (1%)
    all_to_all x1, waiting for transfers between devices, shards(): lax.all_to_all(jnp.stack([scaled] * lax.axis_size('narrow')), 'narrow', 0...  180 us
    reduce_scatter x1, waiting for transfers between devices, shards(): totals = lax.psum_scatter(portion, 'wide', scatter_dimension=0, tiled=True)  85.8 us
    all_gather x1, waiting for transfers between devices, shards(): full_factors = lax.all_gather(factors, 'narrow', axis=1, tiled=True)  44.1 us
    dot_general x1, matrix products, shards(): jnp.einsum('sprv,spmv->sprm', left_rows, right_rows, precision=highest)  25.8 us
    gather x1, local copies, waits for them, and re-layouts, shards(): jnp.concatenate(lax.all_to_all(jnp.stack([scaled] * lax.axis_size('narrow...  12.6 us
    all_to_all x1, local copies, waits for them, and re-layouts, shards(): lax.all_to_all(jnp.stack([scaled] * lax.axis_size('narrow')), 'narrow', 0...  8.46 us
  transfers between devices with their start and end apart: 3, of which 3 were waited for; matrix products, arithmetic and copies ran while one was open for 1% of the time, Pallas kernels for 0%

profile of v1, /device:TPU:2, one launch (start us, length us, event | category | flops | bytes accessed | tf_op | source)
XLA Modules:
  0.0 397.8 jit_solution(17353954467687986533)
XLA Ops:
  6.5 0.0 copy-start
  6.5 0.0 all-gather.2.cloned.1.call-start
  6.5 0.7 all-gather.2.cloned.1.call-update
  7.3 0.8 compare_select_fusion
  8.0 0.1 copy.19
  8.1 0.1 reshape.13
  8.2 0.0 copy-done
  8.2 0.6 gather_fusion
  8.8 44.1 %all-gather.2.cloned.1.call-done = f32[2,512,512]{2,1,0:T(8,128)} async-done(((f32[2,64,512]{2,1,0:T(8,128)}), f32[2,512,512]{2,1,0:T(8,128)}) %all-gather.2.cloned.1.call-update) | async-done | bytes 2097168 | tf_op jit(solution)/shard_map/all_gather | solution.py:30
  53.0 3.5 fusion.8
  56.5 4.3 %stack.2 = f32[8,2,4,64,512]{4,3,2,1,0:T(8,128)} broadcast(f32[2,4,64,512]{3,2,1,0:T(8,128)S(1)} %fusion.8), dimensions={1,2,3,4} | broadcast | bytes 9437184 | tf_op jit(solution)/shard_map/stack | solution.py:35
  60.8 0.0 copy-start.2
  60.8 0.0 copy-start.4
  60.8 0.0 copy-start.3
  60.8 5.1 %all-to-all-start = ((f32[8,2,4,64,512]{4,3,2,1,0:T(8,128)}), f32[8,2,4,64,512]{4,3,2,1,0:T(8,128)}, u32[]{:S(2)}, u32[]{:S(2)}) async-start(f32[8,2,4,64,512]{4,3,2,1,0:T(8,128)} %stack.2), calls=%async_computation | async-start | bytes 16777216 | tf_op jit(solution)/shard_map/all_to_all | solution.py:35
  65.9 0.2 reduce-scatter.2.cloned.1.call-start
  66.2 0.0 copy-done.2
  66.2 0.1 constant_dynamic-slice_fusion
  66.2 0.1 copy.18
  66.3 0.0 copy-done.4
  66.3 0.0 copy-done.3
  66.4 2.2 gather_fusion.1
  68.6 179.8 %all-to-all-done = f32[8,2,4,64,512]{4,3,2,1,0:T(8,128)} async-done(((f32[8,2,4,64,512]{4,3,2,1,0:T(8,128)}), f32[8,2,4,64,512]{4,3,2,1,0:T(8,128)}, u32[]{:S(2)}, u32[]{:S(2)}) %all-to-all-start) | async-done | bytes 8388640 | tf_op jit(solution)/shard_map/all_to_all | solution.py:35
  248.3 8.5 %copy.20 = f32[8,2,4,64,512]{4,3,0,2,1:T(8,128)} copy(f32[8,2,4,64,512]{4,3,2,1,0:T(8,128)} %all-to-all-done) | data formatting | bytes 16777216 | tf_op jit(solution)/shard_map/all_to_all | solution.py:35
  256.8 12.6 %gather_fusion.2 = f32[10,2,512,512]{3,2,1,0:T(8,128)} fusion(f32[2,4,512,512]{3,2,1,0:T(8,128)} %bitcast.24, s32[1024]{0:T(1024)S(1)} %pad_clamp_fusion), kind=kCustom, calls=%fused_computation.2 | custom fusion | bytes 41943080 | tf_op jit(solution)/shard_map/gather | solution.py:34
  269.4 25.8 %fusion = f32[2,10,64,512]{3,2,1,0:T(8,128)S(1)} fusion(f32[10,2,512,512]{3,2,1,0:T(8,128)} %gather_fusion.2, f32[10,2,64,512]{3,2,1,0:T(8,128)} %gather_fusion.1), kind=kOutput, calls=%fused_computation.3 | convolution fusion | flops 4026531840 | bytes 26214400 | tf_op jit(solution)/shard_map/sprv,spmv->sprm/dot_general | solution.py:37
  295.2 3.9 fusion.5
  299.1 4.4 %copy.24 = f32[32,64,512]{2,1,0:T(8,128)} copy(f32[32,64,512]{2,0,1:T(8,128)S(1)} %fusion.5) | data formatting | bytes 8388608 | tf_op jit(solution)/shard_map/spa,sprw->arw/dot_general | solution.py:40
  303.5 0.0 copy-start.1
  303.5 0.0 reduce-scatter.2.cloned.1.call-update
  303.5 85.8 %reduce-scatter.2.cloned.1.call-done = f32[1,64,512]{2,1,0:T(8,128)} async-done(((f32[32,64,512]{2,1,0:T(8,128)}), f32[1,64,512]{2,1,0:T(8,128)}) %reduce-scatter.2.cloned.1.call-update) | async-done | bytes 131088 | tf_op jit(solution)/shard_map/reduce_scatter | solution.py:41
  389.4 0.0 copy-done.1
  389.4 1.6 sub.11
  (3 shorter events, 0.0 us)
Async XLA Ops:
  6.5 1.7 copy-start
  6.5 46.4 %all-gather.2.cloned.1.call-start = ((), (), s32[]{:S(2)}) async-start(), calls=%async_computation.2 | async-start | bytes 2359296 | tf_op jit(solution)/shard_map/all_gather | solution.py:30
  60.8 5.3 %copy-start.2 = (s32[64,10]{0,1:T(8,128)S(1)}, s32[64,10]{0,1:T(8,128)}, u32[]{:S(2)}) copy-start(s32[64,10]{0,1:T(8,128)} %param.12) | copy-start | bytes 7684
  60.8 5.5 %copy-start.4 = (s32[10]{0:T(128)S(1)}, s32[10]{0:T(128)}, u32[]{:S(2)}) copy-start(s32[10]{0:T(128)} %constant.33) | copy-start | bytes 124
  60.8 5.5 %copy-start.3 = (s32[10]{0:T(128)S(1)}, s32[10]{0:T(128)}, u32[]{:S(2)}) copy-start(s32[10]{0:T(128)} %constant.32) | copy-start | bytes 124
  60.8 187.5 %all-to-all-start = ((f32[8,2,4,64,512]{4,3,2,1,0:T(8,128)}), f32[8,2,4,64,512]{4,3,2,1,0:T(8,128)}, u32[]{:S(2)}, u32[]{:S(2)}) async-start(f32[8,2,4,64,512]{4,3,2,1,0:T(8,128)} %stack.2), calls=%async_computation | async-start | bytes 16777216 | tf_op jit(solution)/shard_map/all_to_all | solution.py:35
  65.9 323.4 %reduce-scatter.2.cloned.1.call-start = ((), (), s32[]{:S(2)}) async-start(), calls=%async_computation.3 | async-start | bytes 4325376 | tf_op jit(solution)/shard_map/reduce_scatter | solution.py:41
  303.5 85.9 %copy-start.1 = (f32[1,64,512]{2,1,0:T(8,128)S(1)}, f32[1,64,512]{2,1,0:T(8,128)}, u32[]{:S(2)}) copy-start(f32[1,64,512]{2,1,0:T(8,128)} %param.13) | copy-start | bytes 393220
Sparse Core Ops, SparseCore 0:
  9.1 43.8 all-gather.1
  303.6 85.6 reduce-scatter.1
